TPU v7x, 32 devices: a whole 2x2x4 slice. The times are simulated.
32 devices in a mesh: ctx: 8 (over y, x, core), dp: 4 (over z).
Axes of the slice: x: 2, y: 2, z: 4, core: 2. Of those that a mesh axis runs over, the one named last changes fastest.
Arguments:
- ids: int32 [3072], P('ctx'), may hold values from 0 to 511
- embed_table: bfloat16 [512, 4096], P(None, 'dp'), may hold values from -6 to 6
- norm_gain: bfloat16 [4096], P('dp'), may hold values from 0.25 to 1.75
- w_query: bfloat16 [4096, 4096], P('ctx', 'dp'), may hold values from -0.09375 to 0.09375
- w_key: bfloat16 [4096, 4096], P('ctx', 'dp'), may hold values from -0.09375 to 0.09375
- w_value: bfloat16 [4096, 4096], P('ctx', 'dp'), may hold values from -0.09375 to 0.09375
- short_filter: float32 [3, 3, 4096], P(None, None, 'dp'), may hold values from -4 to 4
- pole_rate: float32 [4096, 16], P('dp'), may hold values from 1.6276042e-05 to 0.05
- residue: float32 [4096, 16], P('dp'), may hold values from -2 to 2
- skip_gain: float32 [4096], P('dp'), may hold values from -4 to 4
- w_out: bfloat16 [4096, 4096], P('ctx', 'dp'), may hold values from -0.09375 to 0.09375
Outputs:
- block_out: bfloat16 [3072, 4096], P('ctx', 'dp')
All inputs are finite; a program needn't handle non-finite values.
Results may differ from a plain program's by a relative error of at most 0.0082.
Values may be sent and summed in bfloat16 or wider, within the bound.
A program may use at most 128 MiB of HBM per device.

v0:
```python
import math
import jax
import jax.numpy as jnp
from jax import lax
from jax.sharding import PartitionSpec as P


def shifted(value, axis, steps):
    count = lax.axis_size(axis)
    initial, last = (max(0, -steps), min(count, count - steps))
    return lax.ppermute(value, axis, [(source, source + steps) for source in range(initial, last)])


def entering_2(value, axis, combine, identity):
    peers, index = (lax.axis_size(axis), lax.axis_index(axis))
    everything = jax.tree.map(lambda part: lax.all_gather(part, axis), value)
    start = jax.tree.map(
        lambda part, zero: jnp.broadcast_to(jnp.asarray(zero, part.dtype), part.shape),
        value,
        identity,
    )

    def turn(k, before):
        reached = k < index
        new = combine(before, jax.tree.map(lambda part: part[k], everything))
        return jax.tree.map(lambda a, b: jnp.where(reached, a, b), new, before)

    return lax.fori_loop(0, peers, turn, start)


def shards(
    ids,
    embed_table,
    norm_gain,
    w_query,
    w_key,
    w_value,
    short_filter,
    pole_rate,
    residue,
    skip_gain,
    w_out,
):
    highest = lax.Precision.HIGHEST
    vocab = embed_table.shape[0]
    channels = w_query.shape[1]
    one_hot = (ids[:, None] == jnp.arange(vocab, dtype=jnp.int32)[None, :]).astype(jnp.bfloat16)
    embedded = jnp.dot(one_hot, embed_table, preferred_element_type=jnp.float32).astype(
        jnp.bfloat16
    )
    full_rows, full_gain = (
        lax.all_gather(embedded, "dp", axis=1, tiled=True),
        lax.all_gather(norm_gain, "dp", axis=0, tiled=True),
    )
    floated = full_rows.astype(jnp.float32)
    scale = lax.rsqrt(jnp.mean(floated * floated, axis=1, keepdims=True) + 1e-06)
    normed = (floated * scale * full_gain.astype(jnp.float32)[None, :]).astype(jnp.bfloat16)
    tok_rows = normed.shape[0]

    def add_rows(piece):
        return jnp.dot(normed, piece, preferred_element_type=jnp.float32)

    query_proj = add_rows(lax.all_gather(w_query, "ctx", axis=0, tiled=True))
    key_proj = add_rows(lax.all_gather(w_key, "ctx", axis=0, tiled=True))
    value_proj = add_rows(lax.all_gather(w_value, "ctx", axis=0, tiled=True))
    projected = jnp.concatenate([query_proj, key_proj, value_proj], axis=1).astype(jnp.bfloat16)
    taps = short_filter.shape[0]
    previous = shifted(projected[tok_rows - (taps - 1) :], "ctx", 1)
    extended = jnp.concatenate([previous, projected], axis=0).astype(jnp.float32)
    filt_rows = short_filter.reshape(taps, 3 * channels)
    convolved = jnp.zeros((tok_rows, 3 * channels), jnp.float32)
    for tap in range(taps):
        convolved = (
            convolved
            + filt_rows[tap][None, :] * extended[taps - 1 - tap : taps - 1 - tap + tok_rows]
        )
    query_conv = convolved[:, :channels]
    gated = convolved[:, channels : 2 * channels] * convolved[:, 2 * channels :]
    sub_len = math.gcd(tok_rows, 64)
    blocks = tok_rows // sub_len
    lag_index = jnp.arange(sub_len, dtype=jnp.int32)
    lags = lag_index.astype(jnp.float32)
    strength = residue * jnp.sqrt(2.0 * pole_rate)
    kernel = jnp.einsum(
        "lck,ck->lc", jnp.exp(-pole_rate[None] * lags[:, None, None]), strength, precision=highest
    )
    offsets = lag_index[:, None] - lag_index[None, :]
    toeplitz = jnp.where((offsets >= 0)[:, :, None], kernel[jnp.maximum(offsets, 0)], 0.0)
    pieces = gated.reshape(blocks, sub_len, channels)
    inside = jnp.einsum("tsc,bsc->btc", toeplitz, pieces, precision=highest)
    tail_decay = jnp.exp(-pole_rate[None] * (sub_len - 1.0 - lags)[:, None, None])
    block_ends = jnp.einsum("sck,bsc->bck", tail_decay, pieces, precision=highest)
    step_decay = jnp.exp(-pole_rate * float(sub_len))

    def advance(state, block_end):
        return (step_decay * state + block_end, state)

    device_end, entering = lax.scan(advance, jnp.zeros_like(step_decay), block_ends)
    device_decay = jnp.exp(-pole_rate * float(tok_rows))

    def combine(earlier, later):
        return (earlier[0] * later[0], later[0] * earlier[1] + later[1])

    decay_total, incoming = entering_2(
        (device_decay, device_end),
        "ctx",
        combine,
        (jnp.ones_like(device_decay), jnp.zeros_like(device_end)),
    )
    block_pos = jnp.arange(blocks, dtype=jnp.float32) * float(sub_len)
    states_in = entering + jnp.exp(-pole_rate[None] * block_pos[:, None, None]) * incoming[None]
    lead = jnp.exp(-pole_rate[None] * (lags + 1.0)[:, None, None]) * strength[None]
    carried = jnp.einsum("tck,bck->btc", lead, states_in, precision=highest)
    long_conv = (inside + carried).reshape(tok_rows, channels) + skip_gain[None, :] * gated
    mixed = (query_conv * long_conv).astype(jnp.bfloat16)
    all_mixed = lax.all_gather(mixed, "dp", axis=1, tiled=True)
    output = jnp.dot(
        all_mixed,
        lax.all_gather(w_out, "ctx", axis=0, tiled=True),
        preferred_element_type=jnp.float32,
    )
    return (embedded.astype(jnp.float32) + output).astype(jnp.bfloat16)


def solution(mesh):
    placed = (
        P("ctx"),
        P(None, "dp"),
        P("dp"),
        P("ctx", "dp"),
        P("ctx", "dp"),
        P("ctx", "dp"),
        P(None, None, "dp"),
        P("dp", None),
        P("dp", None),
        P("dp"),
        P("ctx", "dp"),
    )
    return jax.shard_map(
        shards, mesh=mesh, in_specs=placed, out_specs=P("ctx", "dp"), check_vma=False
    )
```

profile of v0, /device:TPU:0, one launch (start us, length us, event | category | flops | bytes accessed | tf_op | source)
XLA Modules:
  0.0 511.5 jit_solution(16965274444478616923)
XLA Ops:
  13.3 12.5 %multiply_reduce_fusion = f32[1024,64]{1,0:T(8,128)} fusion(f32[1024,16]{1,0:T(8,128)S(1)} %copy.47, f32[64]{0:T(128)S(1)} %iota_convert_fusion, f32[1024,16]{1,0:T(8,128)S(1)} %copy.30), kind=kLoop, calls=%fused_computation.14 | loop fusion | flops 3080192 | bytes 393472
  25.9 14.8 %all_gather.34 = bf16[4096]{0:T(1024)(128)(2,1)S(1)} all-gather(bf16[1024]{0:T(1024)(128)(2,1)S(1)} %copy-done.12), channel_id=1, replica_groups=mesh['ctx'=8,'dp'=4] {'dp'}, dimensions={0}, use_global_device_ids=true | all-gather | bytes 10240 | tf_op jit(solution)/shard_map/all_gather | solution.py:53
  40.7 10.9 %all-gather = f32[8192,16]{0,1:T(8,128)} all-gather(f32[1024,16]{0,1:T(8,128)S(1)} %get-tuple-element.213), channel_id=2, replica_groups=mesh['ctx'=8,'dp'=4] {'ctx'}, dimensions={0}, use_global_device_ids=true | all-gather | bytes 589824 | tf_op jit(solution)/shard_map/all_gather | solution.py:16
  51.6 24.7 %all-gather.9.cloned.1.call-done = bf16[384,4096]{1,0:T(8,128)(2,1)} async-done(((bf16[384,1024]{1,0:T(8,128)(2,1)}), bf16[384,4096]{1,0:T(8,128)(2,1)}) %all-gather.9.cloned.1.call-update) | async-done | bytes 3145744 | tf_op jit(solution)/shard_map/all_gather | solution.py:52
  78.9 52.2 %all-gather.15.cloned.1.call-done = bf16[4096,1024]{1,0:T(8,128)(2,1)} async-done(((bf16[512,1024]{1,0:T(8,128)(2,1)}), bf16[4096,1024]{1,0:T(8,128)(2,1)}) %all-gather.15.cloned.1.call-update) | async-done | bytes 8388624 | tf_op jit(solution)/shard_map/all_gather | solution.py:65
  131.2 7.8 %convolution_convert_fusion = bf16[384,1024]{1,0:T(8,128)(2,1)S(1)} fusion(bf16[4096,1024]{1,0:T(8,128)(2,1)} %all-gather.15.cloned.1.call-done, bf16[384,4096]{1,0:T(8,128)(2,1)} %all-gather.9.cloned.1.call-done, f32[4096]{0:T(1024)S(1)} %convert_element_type.46, f32[384]{0:T(512)S(1)} %add_rsqrt_fusion), kind=kOutput, calls=%fused_computation.45 | convolution fusion | flops 3227910144 | bytes 12338688 | tf_op jit(solution)/shard_map/dot_general | solution.py:61
  139.0 48.4 %all-gather.13.cloned.1.call-done = bf16[4096,1024]{1,0:T(8,128)(2,1)} async-done(((bf16[512,1024]{1,0:T(8,128)(2,1)}), bf16[4096,1024]{1,0:T(8,128)(2,1)}) %all-gather.13.cloned.1.call-update) | async-done | bytes 8388624 | tf_op jit(solution)/shard_map/all_gather | solution.py:64
  187.3 7.8 %convolution_convert_fusion.1 = bf16[384,1024]{1,0:T(8,128)(2,1)S(1)} fusion(bf16[4096,1024]{1,0:T(8,128)(2,1)} %all-gather.13.cloned.1.call-done, bf16[384,4096]{1,0:T(8,128)(2,1)} %all-gather.9.cloned.1.call-done, f32[4096]{0:T(1024)S(1)} %convert_element_type.46, f32[384]{0:T(512)S(1)} %add_rsqrt_fusion), kind=kOutput, calls=%fused_computation.46 | convolution fusion | flops 3227910144 | bytes 12338688 | tf_op jit(solution)/shard_map/dot_general | solution.py:61
  195.1 48.2 %all-gather.11.cloned.1.call-done = bf16[4096,1024]{1,0:T(8,128)(2,1)} async-done(((bf16[512,1024]{1,0:T(8,128)(2,1)}), bf16[4096,1024]{1,0:T(8,128)(2,1)}) %all-gather.11.cloned.1.call-update) | async-done | bytes 8388624 | tf_op jit(solution)/shard_map/all_gather | solution.py:63
  243.4 7.8 %convolution_convert_fusion.2 = bf16[384,1024]{1,0:T(8,128)(2,1)S(1)} fusion(bf16[4096,1024]{1,0:T(8,128)(2,1)} %all-gather.11.cloned.1.call-done, bf16[384,4096]{1,0:T(8,128)(2,1)} %all-gather.9.cloned.1.call-done, f32[4096]{0:T(1024)S(1)} %convert_element_type.46, f32[384]{0:T(512)S(1)} %add_rsqrt_fusion), kind=kOutput, calls=%fused_computation.47 | convolution fusion | flops 3227910144 | bytes 12338688 | tf_op jit(solution)/shard_map/dot_general | solution.py:61
  254.7 18.9 %gather_fusion = f32[4096,1024]{1,0:T(8,128)} fusion(f32[64,1024]{1,0:T(8,128)S(1)} %bitcast.57, s32[4096]{0:T(1024)S(1)} %broadcast_clamp_fusion), kind=kCustom, calls=%fused_computation | custom fusion | bytes 33570816 | tf_op jit(solution)/shard_map/gather | solution.py:88
  273.6 30.7 %copy.31 = f32[64,64,1024]{1,0,2:T(8,128)} copy(f32[64,64,1024]{2,1,0:T(8,128)} %bitcast.58) | data formatting | bytes 33554432 | tf_op jit(solution)/shard_map/gather | solution.py:88
  311.1 2.7 copy.32
  313.8 16.9 %fusion.24 = f32[6,1024,16]{2,0,1:T(8,128)} fusion(f32[6,64,1024]{1,0,2:T(8,128)} %copy.32, f32[64]{0:T(128)S(1)} %broadcast_subtract_fusion, f32[1024,16]{1,0:T(8,128)S(1)} %copy.30), kind=kOutput, calls=%fused_computation.39 | convolution fusion | flops 76546048 | bytes 2031872 | tf_op jit(solution)/shard_map/sck,bsc->bck/dot_general | solution.py:92
  330.7 2.7 copy.34
  333.8 10.3 %all-gather.1 = f32[8192,16]{0,1:T(8,128)S(1)} all-gather(f32[1024,16]{0,1:T(8,128)S(1)} %get-tuple-element.128), channel_id=3, replica_groups=mesh['ctx'=8,'dp'=4] {'ctx'}, dimensions={0}, use_global_device_ids=true | all-gather | bytes 589824 | tf_op jit(solution)/shard_map/all_gather | solution.py:16
  344.3 9.8 %while.28 = (s32[]{:T(128)}, f32[1024,16]{0,1:T(8,128)S(1)}, s32[]{:T(128)}, f32[8,1024,16]{1,0,2:T(8,128)}, f32[8,1024,16]{1,0,2:T(8,128)S(1)}, /*index=5*/s32[]{:T(128)}, s32[]{:T(128)}) while((s32[]{:T(128)}, f32[1024,16]{0,1:T(8,128)S(1)}, s32[]{:T(128)}, f32[8,1024,16]{1,0,2:T(8,128)}, f32[8,1024,16]{1,0,2:T(8,128)S(1)}, ...), condition=%wide.region_4.5_spmd.clone, body=%wide.region_3.4_spmd.clone.sunk | while | flops 65540 | bytes 524397 | solution.py:28
  354.2 2.7 copy.38
  356.9 56.2 %fusion.3 = f32[1024,6,64]{2,1,0:T(8,128)S(1)} fusion(f32[6,64,1024]{1,0,2:T(8,128)} %copy.32, f32[64,64,1024]{1,0,2:T(8,128)} %copy.31, pred[64,64]{1,0:T(8,128)(4,1)S(1)} %subtract_compare_fusion), kind=kOutput, calls=%fused_computation.10 | convolution fusion | flops 306184192 | bytes 19927040 | tf_op jit(solution)/shard_map/tsc,bsc->btc/dot_general | solution.py:90
  413.2 12.3 %add_bitcast_fusion = f32[6,64,1024]{1,0,2:T(8,128)} fusion(f32[1024,6,64]{2,1,0:T(8,128)S(1)} %fusion.3, f32[6,1024,16]{2,0,1:T(8,128)S(1)} %copy-done.3, f32[1024,16]{1,0:T(8,128)S(1)} %copy-done.6, f32[64]{0:T(128)S(1)} %broadcast_add_fusion, f32[1024,16]{1,0:T(8,128)S(1)} %copy.30), kind=kOutput, calls=%fused_computation.32 | convolution fusion | flops 77987840 | bytes 3670272 | tf_op jit(solution)/shard_map/tck,bck->btc/dot_general | solution.py:113
  425.5 2.7 copy.39
  428.2 3.9 fusion.29
  432.2 63.5 %all-gather.17.cloned.1.call-done = bf16[384,4096]{1,0:T(8,128)(2,1)} async-done(((bf16[384,1024]{1,0:T(8,128)(2,1)}), bf16[384,4096]{1,0:T(8,128)(2,1)}) %all-gather.17.cloned.1.call-update) | async-done | bytes 3145744 | tf_op jit(solution)/shard_map/all_gather | solution.py:116
  495.8 8.7 %add_convert_fusion = bf16[384,1024]{1,0:T(8,128)(2,1)} fusion(bf16[384,1024]{1,0:T(8,128)(2,1)S(1)} %copy-done.4, bf16[384,4096]{1,0:T(8,128)(2,1)} %all-gather.17.cloned.1.call-done, bf16[4096,1024]{1,0:T(8,128)(2,1)} %all-gather.19.cloned.1.call-done), kind=kOutput, calls=%fused_computation.44 | convolution fusion | flops 3222405120 | bytes 13107200 | tf_op jit(solution)/shard_map/dot_general | solution.py:117
  (100 shorter events, 30.0 us)
Async XLA Ops:
  6.5 1.2 copy-start
  6.5 6.2 %copy-start.10 = (f32[3,3,1024]{2,1,0:T(4,128)S(1)}, f32[3,3,1024]{2,1,0:T(4,128)}, u32[]{:S(2)}) copy-start(f32[3,3,1024]{2,1,0:T(4,128)} %param.21) | copy-start | bytes 110596
  6.5 6.2 %copy-start.8 = (f32[1024,16]{0,1:T(8,128)S(1)}, f32[1024,16]{0,1:T(8,128)}, u32[]{:S(2)}) copy-start(f32[1024,16]{0,1:T(8,128)} %param.22) | copy-start | bytes 196612
  6.5 6.2 %copy-start.9 = (f32[1024,16]{0,1:T(8,128)S(1)}, f32[1024,16]{0,1:T(8,128)}, u32[]{:S(2)}) copy-start(f32[1024,16]{0,1:T(8,128)} %param.23) | copy-start | bytes 196612
  6.5 69.8 %all-gather.9.cloned.1.call-start = ((), (), s32[]{:S(2)}) async-start(), calls=%async_computation | async-start | bytes 3932160 | tf_op jit(solution)/shard_map/all_gather | solution.py:52
  9.9 15.9 %copy-start.12 = (bf16[1024]{0:T(1024)(128)(2,1)S(1)}, bf16[1024]{0:T(1024)(128)(2,1)}, u32[]{:S(2)}) copy-start(bf16[1024]{0:T(1024)(128)(2,1)} %param.17) | copy-start | bytes 6148
  10.0 121.2 %all-gather.15.cloned.1.call-start = ((), (), s32[]{:S(2)}) async-start(), calls=%async_computation.3 | async-start | bytes 9437184 | tf_op jit(solution)/shard_map/all_gather | solution.py:65
  10.7 176.6 %all-gather.13.cloned.1.call-start = ((), (), s32[]{:S(2)}) async-start(), calls=%async_computation.2 | async-start | bytes 9437184 | tf_op jit(solution)/shard_map/all_gather | solution.py:64
  11.5 231.9 %all-gather.11.cloned.1.call-start = ((), (), s32[]{:S(2)}) async-start(), calls=%async_computation.1 | async-start | bytes 9437184 | tf_op jit(solution)/shard_map/all_gather | solution.py:63
  12.0 420.2 %all-gather.19.cloned.1.call-start = ((), (), s32[]{:S(2)}) async-start(), calls=%async_computation.5 | async-start | bytes 9437184 | tf_op jit(solution)/shard_map/all_gather | solution.py:119
  12.6 483.1 %all-gather.17.cloned.1.call-start = ((), (), s32[]{:S(2)}) async-start(), calls=%async_computation.4 | async-start | bytes 3932160 | tf_op jit(solution)/shard_map/all_gather | solution.py:116
  13.0 65.9 %copy-start.5 = (f32[1024,16]{1,0:T(8,128)}, f32[1024,16]{1,0:T(8,128)S(1)}, u32[]{:S(2)}) copy-start(f32[1024,16]{1,0:T(8,128)S(1)} %copy.47) | copy-start | bytes 196612
  251.2 55.3 %collective-permute-start = (bf16[2,3072]{1,0:T(2,128)(2,1)S(1)}, bf16[2,3072]{1,0:T(2,128)(2,1)S(1)}, u32[]{:S(2)}, u32[]{:S(2)}) collective-permute-start(bf16[2,3072]{1,0:T(2,128)(2,1)S(1)} %pad_maximum_fusion), channel_id=1, source_target_pairs={{0,4},{4,8},{8,12},{12,16},{16,20},{20,24},{24,28},{1,5},{5,9},{9,... | collective-permute-start | bytes 36872 | tf_op jit(solution)/shard_map/ppermute | solution.py:11
  308.6 2.2 copy-start.2
  313.8 19.5 %copy-start.7 = (f32[6,1024,16]{1,2,0:T(8,128)S(1)}, f32[6,1024,16]{1,2,0:T(8,128)}, u32[]{:S(2)}) copy-start(f32[6,1024,16]{1,2,0:T(8,128)} %custom-call.4) | copy-start | bytes 1179652
  356.9 56.2 %copy-start.3 = (f32[6,1024,16]{2,0,1:T(8,128)S(1)}, f32[6,1024,16]{2,0,1:T(8,128)}, u32[]{:S(2)}) copy-start(f32[6,1024,16]{2,0,1:T(8,128)} %copy.38) | copy-start | bytes 1179652
  356.9 56.2 %copy-start.6 = (f32[1024,16]{1,0:T(8,128)S(1)}, f32[1024,16]{1,0:T(8,128)}, u32[]{:S(2)}) copy-start(f32[1024,16]{1,0:T(8,128)} %copy-done.5) | copy-start | bytes 196612
  425.5 2.7 copy-start.11
  428.2 67.5 %copy-start.4 = (bf16[384,1024]{1,0:T(8,128)(2,1)S(1)}, bf16[384,1024]{1,0:T(8,128)(2,1)}, u32[]{:S(2)}) copy-start(bf16[384,1024]{1,0:T(8,128)(2,1)} %convolution_convert_fusion.3) | copy-start | bytes 2359300
  495.8 8.7 %copy-start.1 = (bf16[512,1024]{1,0:T(8,128)(2,1)S(1)}, bf16[512,1024]{1,0:T(8,128)(2,1)}, u32[]{:S(2)}) copy-start(bf16[512,1024]{1,0:T(8,128)(2,1)} %param.16) | copy-start | bytes 3145732
Sparse Core Ops, SparseCore 0:
  10.1 66.2 all-gather.8
  78.2 52.8 all-gather.14
  133.0 54.2 all-gather.12
  189.1 54.2 all-gather.10
  245.1 54.2 all-gather.18
  432.3 63.4 all-gather.16
where the time goes:
time: 521 us; the launch traced here: 512 us
  waiting for transfers between devices  240 us (46%)
  matrix products  120 us (23%)
  local copies, waits for them, and re-layouts  77.3 us (15%)
  blocking collectives  36 us (7%)
  other arithmetic  22.2 us (4%)
  between operations  14 us (3%)
    all_gather x1, waiting for transfers between devices, shards(): all_mixed = lax.all_gather(mixed, 'dp', axis=1, tiled=True)  63.5 us
    dot_general x1, matrix products, shards(): inside = jnp.einsum('tsc,bsc->btc', toeplitz, pieces, precision=highest)  56.2 us
    all_gather x1, waiting for transfers between devices, shards(): value_proj = add_rows(lax.all_gather(w_value, 'ctx', axis=0, tiled=True))  52.2 us
    gather x2, local copies, waits for them, and re-layouts, shards(): kernel[jnp.maximum(offsets, 0)]  49.6 us
    all_gather x1, waiting for transfers between devices, shards(): key_proj = add_rows(lax.all_gather(w_key, 'ctx', axis=0, tiled=True))  48.4 us
    all_gather x1, waiting for transfers between devices, shards(): query_proj = add_rows(lax.all_gather(w_query, 'ctx', axis=0, tiled=True))  48.2 us
    all_gather x1, waiting for transfers between devices, shards(): lax.all_gather(embedded, 'dp', axis=1, tiled=True)  24.7 us
    dot_general x3, matrix products, add_rows(): return jnp.dot(normed, piece, preferred_element_type=jnp.float32)  23.4 us
  transfers between devices with their start and end apart: 7, of which 5 were waited for; matrix products, arithmetic and copies ran while one was open for 40% of the time, Pallas kernels for 0%

commit v1 on v0

--- a/solution.py
+++ b/solution.py
@@ -3,6 +3,7 @@
 import jax.numpy as jnp
 from jax import lax
 from jax.sharding import PartitionSpec as P
+from jax.lax import all_to_all, axis_size
 
 
 def shifted(value, axis, steps):
@@ -60,7 +61,18 @@
     def add_rows(piece):
         return jnp.dot(normed, piece, preferred_element_type=jnp.float32)
 
-    query_proj = add_rows(lax.all_gather(w_query, "ctx", axis=0, tiled=True))
+    def fill_domain(z_in):
+        axis_id = "ctx"
+        sides = axis_size(axis_id)
+        return all_to_all(
+            jnp.tile(z_in, list(map(lambda pp: sides if pp == 0 else 1, range(z_in.ndim)))),
+            axis_id,
+            split_axis=0,
+            concat_axis=0,
+            tiled=True,
+        )
+
+    query_proj = add_rows(fill_domain(w_query))
     key_proj = add_rows(lax.all_gather(w_key, "ctx", axis=0, tiled=True))
     value_proj = add_rows(lax.all_gather(w_value, "ctx", axis=0, tiled=True))
     projected = jnp.concatenate([query_proj, key_proj, value_proj], axis=1).astype(jnp.bfloat16)

time: 521 us -> 482 us (0.925)
  waiting for transfers between devices: 240 us -> 119 us
  blocking collectives: 36 us -> 113 us
  starting transfers between devices: 2.38 us -> 7.65 us
    all_gather x2, blocking collectives: 21.1 us -> 98.6 us  [entering_2(): everything = jax.tree.map(lambda part: lax.all_gather(part, axis), value)]
    all_gather x1 -> x0, waiting for transfers between devices: 48.2 us -> none  [shards(): query_proj = add_rows(lax.all_gather(w_query, 'ctx', axis=0, tiled=True))]
    all_gather x1, waiting for transfers between devices: 52.2 us -> 4.74 us  [shards(): value_proj = add_rows(lax.all_gather(w_value, 'ctx', axis=0, tiled=True))]
    all_gather x1, waiting for transfers between devices: 24.7 us -> 0.01 us  [shards(): lax.all_gather(embedded, 'dp', axis=1, tiled=True)]
    all_to_all x0 -> x1, starting transfers between devices: none -> 5.33 us  [fill_domain(): all_to_all(jnp.tile(z_in, list(map(lambda pp: sides if pp == 0 else 1, ra...]
  transfers between devices with their start and end apart: 7 -> 7, of which waited for: 5 -> 3; matrix products, arithmetic and copies ran while one was open for 40% -> 44% of each run, Pallas kernels for 0% -> 0%
where the time goes in v1:
time: 482 us; the launch traced here: 477 us
  matrix products  120 us (25%)
  waiting for transfers between devices  119 us (25%)
  blocking collectives  113 us (23%)
  local copies, waits for them, and re-layouts  81.5 us (17%)
  other arithmetic  22.2 us (5%)
  between operations  13.7 us (3%)
  starting transfers between devices  7.65 us (2%)
    all_gather x2, blocking collectives, entering_2(): everything = jax.tree.map(lambda part: lax.all_gather(part, axis), value)  98.6 us
    all_gather x1, waiting for transfers between devices, shards(): all_mixed = lax.all_gather(mixed, 'dp', axis=1, tiled=True)  63.5 us
    dot_general x1, matrix products, shards(): inside = jnp.einsum('tsc,bsc->btc', toeplitz, pieces, precision=highest)  56.2 us
    gather x2, local copies, waits for them, and re-layouts, shards(): kernel[jnp.maximum(offsets, 0)]  49.5 us
    all_gather x1, waiting for transfers between devices, shards(): key_proj = add_rows(lax.all_gather(w_key, 'ctx', axis=0, tiled=True))  49.1 us
    dot_general x3, matrix products, add_rows(): return jnp.dot(normed, piece, preferred_element_type=jnp.float32)  23.4 us
    dot_general x1, matrix products, shards(): jnp.einsum('sck,bsc->bck', tail_decay, pieces, precision=highest)  16.9 us
    all_gather x1, blocking collectives, shards(): lax.all_gather(norm_gain, 'dp', axis=0, tiled=True)  14.2 us
  transfers between devices with their start and end apart: 7, of which 3 were waited for; matrix products, arithmetic and copies ran while one was open for 44% of the time, Pallas kernels for 0%

profile of v1, /device:TPU:0, one launch (start us, length us, event | category | flops | bytes accessed | tf_op | source)
XLA Modules:
  0.0 477.3 jit_solution(15558252561068745203)
XLA Ops:
  11.5 4.3 tile.2
  15.8 5.3 %all-to-all-start = ((bf16[8,512,1024]{2,1,0:T(8,128)(2,1)}), bf16[8,512,1024]{2,1,0:T(8,128)(2,1)}, u32[]{:S(2)}, u32[]{:S(2)}) async-start(bf16[8,512,1024]{2,1,0:T(8,128)(2,1)} %tile.2), calls=%async_computation | async-start | bytes 16777216 | tf_op jit(solution)/shard_map/all_to_all | solution.py:67
  22.4 12.6 %multiply_reduce_fusion = f32[1024,64]{1,0:T(8,128)} fusion(f32[1024,16]{1,0:T(8,128)S(1)} %copy.47, f32[64]{0:T(128)S(1)} %iota_convert_fusion, f32[1024,16]{1,0:T(8,128)S(1)} %copy.30), kind=kLoop, calls=%fused_computation.14 | loop fusion | flops 3080192 | bytes 393472
  35.0 14.2 %all_gather.31 = bf16[4096]{0:T(1024)(128)(2,1)S(1)} all-gather(bf16[1024]{0:T(1024)(128)(2,1)S(1)} %copy-done.13), channel_id=1, replica_groups=mesh['ctx'=8,'dp'=4] {'dp'}, dimensions={0}, use_global_device_ids=true | all-gather | bytes 10240 | tf_op jit(solution)/shard_map/all_gather | solution.py:54
  49.1 88.5 %all-gather = f32[8192,16]{0,1:T(8,128)} all-gather(f32[1024,16]{0,1:T(8,128)S(1)} %get-tuple-element.213), channel_id=2, replica_groups=mesh['ctx'=8,'dp'=4] {'ctx'}, dimensions={0}, use_global_device_ids=true | all-gather | bytes 589824 | tf_op jit(solution)/shard_map/all_gather | solution.py:17
  140.2 7.8 %convolution_convert_fusion.2 = bf16[384,1024]{1,0:T(8,128)(2,1)S(1)} fusion(bf16[4096,1024]{1,0:T(8,128)(2,1)} %bitcast.1, bf16[384,4096]{1,0:T(8,128)(2,1)} %all-gather.8.cloned.1.call-done, f32[4096]{0:T(1024)S(1)} %convert_element_type.46, f32[384]{0:T(512)S(1)} %add_rsqrt_fusion), kind=kOutput, calls=%fused_computation.47 | convolution fusion | flops 3227910144 | bytes 12338688 | tf_op jit(solution)/shard_map/dot_general | solution.py:62
  148.0 4.7 all-gather.12.cloned.1.call-done
  152.8 7.8 %convolution_convert_fusion = bf16[384,1024]{1,0:T(8,128)(2,1)S(1)} fusion(bf16[4096,1024]{1,0:T(8,128)(2,1)} %all-gather.12.cloned.1.call-done, bf16[384,4096]{1,0:T(8,128)(2,1)} %all-gather.8.cloned.1.call-done, f32[4096]{0:T(1024)S(1)} %convert_element_type.46, f32[384]{0:T(512)S(1)} %add_rsqrt_fusion), kind=kOutput, calls=%fused_computation.45 | convolution fusion | flops 3227910144 | bytes 12338688 | tf_op jit(solution)/shard_map/dot_general | solution.py:62
  160.6 49.1 %all-gather.10.cloned.1.call-done = bf16[4096,1024]{1,0:T(8,128)(2,1)} async-done(((bf16[512,1024]{1,0:T(8,128)(2,1)}), bf16[4096,1024]{1,0:T(8,128)(2,1)}) %all-gather.10.cloned.1.call-update) | async-done | bytes 8388624 | tf_op jit(solution)/shard_map/all_gather | solution.py:76
  209.7 7.8 %convolution_convert_fusion.1 = bf16[384,1024]{1,0:T(8,128)(2,1)S(1)} fusion(bf16[4096,1024]{1,0:T(8,128)(2,1)} %all-gather.10.cloned.1.call-done, bf16[384,4096]{1,0:T(8,128)(2,1)} %all-gather.8.cloned.1.call-done, f32[4096]{0:T(1024)S(1)} %convert_element_type.46, f32[384]{0:T(512)S(1)} %add_rsqrt_fusion), kind=kOutput, calls=%fused_computation.46 | convolution fusion | flops 3227910144 | bytes 12338688 | tf_op jit(solution)/shard_map/dot_general | solution.py:62
  221.0 18.6 %gather_fusion = f32[4096,1024]{1,0:T(8,128)} fusion(f32[64,1024]{1,0:T(8,128)S(1)} %bitcast.58, s32[4096]{0:T(1024)S(1)} %broadcast_clamp_fusion), kind=kCustom, calls=%fused_computation | custom fusion | bytes 33570816 | tf_op jit(solution)/shard_map/gather | solution.py:100
  239.6 30.9 %copy.31 = f32[64,64,1024]{1,0,2:T(8,128)} copy(f32[64,64,1024]{2,1,0:T(8,128)} %bitcast.59) | data formatting | bytes 33554432 | tf_op jit(solution)/shard_map/gather | solution.py:100
  277.2 2.7 copy.32
  280.0 16.9 %fusion.24 = f32[6,1024,16]{2,0,1:T(8,128)} fusion(f32[6,64,1024]{1,0,2:T(8,128)} %copy.32, f32[64]{0:T(128)S(1)} %broadcast_subtract_fusion, f32[1024,16]{1,0:T(8,128)S(1)} %copy.30), kind=kOutput, calls=%fused_computation.39 | convolution fusion | flops 76546048 | bytes 2031872 | tf_op jit(solution)/shard_map/sck,bsc->bck/dot_general | solution.py:104
  296.8 2.7 copy.34
  299.9 10.2 %all-gather.1 = f32[8192,16]{0,1:T(8,128)S(1)} all-gather(f32[1024,16]{0,1:T(8,128)S(1)} %get-tuple-element.128), channel_id=3, replica_groups=mesh['ctx'=8,'dp'=4] {'ctx'}, dimensions={0}, use_global_device_ids=true | all-gather | bytes 589824 | tf_op jit(solution)/shard_map/all_gather | solution.py:17
  310.4 9.8 %while.28 = (s32[]{:T(128)}, f32[1024,16]{0,1:T(8,128)S(1)}, s32[]{:T(128)}, f32[8,1024,16]{1,0,2:T(8,128)}, f32[8,1024,16]{1,0,2:T(8,128)S(1)}, /*index=5*/s32[]{:T(128)}, s32[]{:T(128)}) while((s32[]{:T(128)}, f32[1024,16]{0,1:T(8,128)S(1)}, s32[]{:T(128)}, f32[8,1024,16]{1,0,2:T(8,128)}, f32[8,1024,16]{1,0,2:T(8,128)S(1)}, ...), condition=%wide.region_4.5_spmd.clone, body=%wide.region_3.4_spmd.clone.sunk | while | flops 65540 | bytes 524397 | solution.py:29
  320.3 2.7 copy.38
  323.0 56.2 %fusion.3 = f32[1024,6,64]{2,1,0:T(8,128)S(1)} fusion(f32[6,64,1024]{1,0,2:T(8,128)} %copy.32, f32[64,64,1024]{1,0,2:T(8,128)} %copy.31, pred[64,64]{1,0:T(8,128)(4,1)S(1)} %subtract_compare_fusion), kind=kOutput, calls=%fused_computation.10 | convolution fusion | flops 306184192 | bytes 19927040 | tf_op jit(solution)/shard_map/tsc,bsc->btc/dot_general | solution.py:102
  379.2 12.4 %add_bitcast_fusion = f32[6,64,1024]{1,0,2:T(8,128)} fusion(f32[1024,6,64]{2,1,0:T(8,128)S(1)} %fusion.3, f32[6,1024,16]{2,0,1:T(8,128)S(1)} %copy-done.3, f32[1024,16]{1,0:T(8,128)S(1)} %copy-done.7, f32[64]{0:T(128)S(1)} %broadcast_add_fusion, f32[1024,16]{1,0:T(8,128)S(1)} %copy.30), kind=kOutput, calls=%fused_computation.32 | convolution fusion | flops 77987840 | bytes 3670272 | tf_op jit(solution)/shard_map/tck,bck->btc/dot_general | solution.py:125
  391.6 2.7 copy.39
  394.3 3.9 fusion.29
  398.3 63.5 %all-gather.14.cloned.1.call-done = bf16[384,4096]{1,0:T(8,128)(2,1)} async-done(((bf16[384,1024]{1,0:T(8,128)(2,1)}), bf16[384,4096]{1,0:T(8,128)(2,1)}) %all-gather.14.cloned.1.call-update) | async-done | bytes 3145744 | tf_op jit(solution)/shard_map/all_gather | solution.py:128
  461.8 8.7 %add_convert_fusion = bf16[384,1024]{1,0:T(8,128)(2,1)} fusion(bf16[384,1024]{1,0:T(8,128)(2,1)S(1)} %copy-done.5, bf16[384,4096]{1,0:T(8,128)(2,1)} %all-gather.14.cloned.1.call-done, bf16[4096,1024]{1,0:T(8,128)(2,1)} %all-gather.16.cloned.1.call-done), kind=kOutput, calls=%fused_computation.44 | convolution fusion | flops 3222405120 | bytes 13107200 | tf_op jit(solution)/shard_map/dot_general | solution.py:129
  (102 shorter events, 29.4 us)
Async XLA Ops:
  6.5 1.2 copy-start
  6.5 4.9 %copy-start.4 = (bf16[512,1024]{1,0:T(8,128)(2,1)S(1)}, bf16[512,1024]{1,0:T(8,128)(2,1)}, u32[]{:S(2)}) copy-start(bf16[512,1024]{1,0:T(8,128)(2,1)} %param.18) | copy-start | bytes 3145732
  6.5 131.0 %all-gather.8.cloned.1.call-start = ((), (), s32[]{:S(2)}) async-start(), calls=%async_computation.1 | async-start | bytes 3932160 | tf_op jit(solution)/shard_map/all_gather | solution.py:53
  10.0 142.8 %all-gather.12.cloned.1.call-start = ((), (), s32[]{:S(2)}) async-start(), calls=%async_computation.3 | async-start | bytes 9437184 | tf_op jit(solution)/shard_map/all_gather | solution.py:77
  10.7 198.9 %all-gather.10.cloned.1.call-start = ((), (), s32[]{:S(2)}) async-start(), calls=%async_computation.2 | async-start | bytes 9437184 | tf_op jit(solution)/shard_map/all_gather | solution.py:76
  15.8 6.0 %copy-start.9 = (f32[1024,16]{0,1:T(8,128)S(1)}, f32[1024,16]{0,1:T(8,128)}, u32[]{:S(2)}) copy-start(f32[1024,16]{0,1:T(8,128)} %param.22) | copy-start | bytes 196612
  15.8 6.0 %copy-start.10 = (f32[1024,16]{0,1:T(8,128)S(1)}, f32[1024,16]{0,1:T(8,128)}, u32[]{:S(2)}) copy-start(f32[1024,16]{0,1:T(8,128)} %param.23) | copy-start | bytes 196612
  15.8 6.6 %copy-start.11 = (f32[3,3,1024]{2,1,0:T(4,128)S(1)}, f32[3,3,1024]{2,1,0:T(4,128)}, u32[]{:S(2)}) copy-start(f32[3,3,1024]{2,1,0:T(4,128)} %param.21) | copy-start | bytes 110596
  15.8 124.4 %all-to-all-start = ((bf16[8,512,1024]{2,1,0:T(8,128)(2,1)}), bf16[8,512,1024]{2,1,0:T(8,128)(2,1)}, u32[]{:S(2)}, u32[]{:S(2)}) async-start(bf16[8,512,1024]{2,1,0:T(8,128)(2,1)} %tile.2), calls=%async_computation | async-start | bytes 16777216 | tf_op jit(solution)/shard_map/all_to_all | solution.py:67
  21.1 13.8 %copy-start.13 = (bf16[1024]{0:T(1024)(128)(2,1)S(1)}, bf16[1024]{0:T(1024)(128)(2,1)}, u32[]{:S(2)}) copy-start(bf16[1024]{0:T(1024)(128)(2,1)} %param.17) | copy-start | bytes 6148
  21.1 377.1 %all-gather.16.cloned.1.call-start = ((), (), s32[]{:S(2)}) async-start(), calls=%async_computation.5 | async-start | bytes 9437184 | tf_op jit(solution)/shard_map/all_gather | solution.py:131
  21.7 440.1 %all-gather.14.cloned.1.call-start = ((), (), s32[]{:S(2)}) async-start(), calls=%async_computation.4 | async-start | bytes 3932160 | tf_op jit(solution)/shard_map/all_gather | solution.py:128
  22.0 118.2 %copy-start.6 = (f32[1024,16]{1,0:T(8,128)}, f32[1024,16]{1,0:T(8,128)S(1)}, u32[]{:S(2)}) copy-start(f32[1024,16]{1,0:T(8,128)S(1)} %copy.47) | copy-start | bytes 196612
  217.5 55.1 %collective-permute-start = (bf16[2,3072]{1,0:T(2,128)(2,1)S(1)}, bf16[2,3072]{1,0:T(2,128)(2,1)S(1)}, u32[]{:S(2)}, u32[]{:S(2)}) collective-permute-start(bf16[2,3072]{1,0:T(2,128)(2,1)S(1)} %pad_maximum_fusion), channel_id=1, source_target_pairs={{0,4},{4,8},{8,12},{12,16},{16,20},{20,24},{24,28},{1,5},{5,9},{9,... | collective-permute-start | bytes 36872 | tf_op jit(solution)/shard_map/ppermute | solution.py:12
  274.7 2.2 copy-start.2
  280.0 19.5 %copy-start.8 = (f32[6,1024,16]{1,2,0:T(8,128)S(1)}, f32[6,1024,16]{1,2,0:T(8,128)}, u32[]{:S(2)}) copy-start(f32[6,1024,16]{1,2,0:T(8,128)} %custom-call.4) | copy-start | bytes 1179652
  323.0 56.2 %copy-start.3 = (f32[6,1024,16]{2,0,1:T(8,128)S(1)}, f32[6,1024,16]{2,0,1:T(8,128)}, u32[]{:S(2)}) copy-start(f32[6,1024,16]{2,0,1:T(8,128)} %copy.38) | copy-start | bytes 1179652
  323.0 56.2 %copy-start.7 = (f32[1024,16]{1,0:T(8,128)S(1)}, f32[1024,16]{1,0:T(8,128)}, u32[]{:S(2)}) copy-start(f32[1024,16]{1,0:T(8,128)} %copy-done.6) | copy-start | bytes 196612
  391.6 2.7 copy-start.12
  394.3 67.5 %copy-start.5 = (bf16[384,1024]{1,0:T(8,128)(2,1)S(1)}, bf16[384,1024]{1,0:T(8,128)(2,1)}, u32[]{:S(2)}) copy-start(bf16[384,1024]{1,0:T(8,128)(2,1)} %convolution_convert_fusion.3) | copy-start | bytes 2359300
  461.8 8.7 %copy-start.1 = (bf16[512,1024]{1,0:T(8,128)(2,1)S(1)}, bf16[512,1024]{1,0:T(8,128)(2,1)}, u32[]{:S(2)}) copy-start(bf16[512,1024]{1,0:T(8,128)(2,1)} %param.16) | copy-start | bytes 3145732
Sparse Core Ops, SparseCore 0:
  10.1 66.2 all-gather.7
  78.3 74.4 all-gather.11
  154.7 54.9 all-gather.9
  211.4 54.2 all-gather.15
  398.4 63.4 all-gather.13
